TPU v7x, 128 devices: a whole 4x4x4 slice. The times are simulated.
128 devices in a mesh: section: 2 (over z_hi), seq: 8 (over x, z_lo), expert: 8 (over y, core).
Axes of the slice: x: 4, y: 4, z: 4 (z_hi: 2, z_lo: 2; z = z_hi * 2 + z_lo), core: 2. Of those that a mesh axis runs over, the one named last changes fastest.
Arguments:
- tokens: bfloat16 [2, 1024, 2048], P(None, ('seq', 'expert')), may hold values from -12 to 12
- prompt_lengths: int32 [2, 3], replicated, may hold values from 1 to 512, 1024 in all within a row
- cache_lengths: int32 [2, 3], replicated, may hold values from 1 to 1024, 2048 in all within a row
- kv_cache: bfloat16 [2, 2048, 2, 2048], P(None, 'seq', None, 'expert'), may hold values from -360 to 360
- attn_routes: int32 [2, 1024, 2], P(None, 'seq'), may hold values from 0 to 3, all different within a row
- ffn_routes: int32 [2, 1024, 2], P(None, ('seq', 'expert')), may hold values from 0 to 7, all different within a row; in each aligned block of 16 rows (0 to 15, 16 to 31, ..., all dimensions but the last counted through in order) at most 8 rows name the same one
- attn_gain: float32 [2048], replicated, may hold values from 0.1 to 1.9
- ffn_gain: float32 [2048], replicated, may hold values from 0.1 to 1.9
- attn_mix: bfloat16 [2048, 4], replicated, may hold values from -0.125 to 0.125
- query_weight: bfloat16 [2048, 4, 2048], P(None, None, 'expert'), may hold values from -0.125 to 0.125
- kv_weight: bfloat16 [2048, 2, 2048], P(None, None, 'expert'), may hold values from -0.125 to 0.125
- out_weight: bfloat16 [4, 2048, 2048], P(None, 'expert'), may hold values from -0.125 to 0.125
- ffn_mix: bfloat16 [2048, 8], replicated, may hold values from -0.125 to 0.125
- in_weight: bfloat16 [8, 2048, 2, 5632], P('expert', None, None, 'seq'), may hold values from -0.125 to 0.125
- down_weight: bfloat16 [8, 5632, 2048], P('expert', 'seq'), may hold values from -0.078125 to 0.078125
Outputs:
- layer_out: bfloat16 [2, 1024, 2048], P('section', ('seq', 'expert'))
Inputs may be any that keep to these rules, and one draw needn't show every extreme that they name: `prompt_lengths`: each row sums to 1024; its largest entry is 512. `cache_lengths`: each row sums to 2048; its largest entry is 1024. `attn_routes`: the two experts of a position differ; every expert is named somewhere. `ffn_routes`: the two experts of a position differ. Taking all micro-batches and positions in order, in each aligned block of 16 positions (the rows of one device) no expert is named more than 8 times, and some block names one exactly 8 times.
All inputs are finite; a program needn't handle non-finite values.
Results may differ from a plain program's by a relative error of at most 0.029.
Values may be sent and summed in bfloat16 or wider, within the bound.
A program may use at most 128 MiB of HBM per device.

v0:
```python
import jax
import jax.numpy as jnp
from jax import lax
from jax.sharding import PartitionSpec as P

HEAD_DIM = 128
EPS = 1e-06
THETA = 10000.0
NEGATIVE = -1e30


def rms_scale(values, gain):
    widened = values.astype(jnp.float32)
    inverse = lax.rsqrt(jnp.mean(widened * widened, axis=-1, keepdims=True) + EPS)
    return (widened * inverse * gain).astype(jnp.bfloat16)


def segment_of(row_index, lengths):
    ends = jnp.cumsum(lengths)
    return jnp.sum((row_index[:, None] >= ends[None, :]).astype(jnp.int32), axis=1)


def positions(row_index, lengths, cached):
    ends = jnp.cumsum(lengths)
    segment = jnp.sum((row_index[:, None] >= ends[None, :]).astype(jnp.int32), axis=1)
    matched = segment[:, None] == jnp.arange(lengths.shape[0], dtype=jnp.int32)[None, :]
    begins = jnp.sum(jnp.where(matched, (ends - lengths)[None, :], 0), axis=1)
    offsets = jnp.sum(jnp.where(matched, cached[None, :], 0), axis=1)
    return (segment, offsets + row_index - begins)


def rotate(values, place):
    half_dim = values.shape[-1] // 2
    freq = THETA ** (-jnp.arange(half_dim, dtype=jnp.float32) / half_dim)
    angle = place.astype(jnp.float32)[:, None] * freq[None, :]
    shape = (values.shape[0],) + (1,) * (values.ndim - 2) + (half_dim,)
    cosine = jnp.cos(angle).reshape(shape)
    sine = jnp.sin(angle).reshape(shape)
    former = values[..., :half_dim]
    latter = values[..., half_dim:]
    return jnp.concatenate(
        [former * cosine - latter * sine, latter * cosine + former * sine], axis=-1
    )


def route_gates(normed, mixing, routes):
    logits = jnp.dot(normed, mixing, preferred_element_type=jnp.float32)
    chosen = jnp.take_along_axis(logits, routes, axis=1)
    leading = jax.nn.sigmoid(chosen[:, 0] - chosen[:, 1])
    return jnp.stack([leading, 1.0 - leading], axis=1)


def select_batch(values, batch):
    return lax.dynamic_index_in_dim(values, batch, 0, keepdims=False)


def attention_block(
    own_rows, lengths, cached, cache_rows, routes, gain, mixing, query_weight, kv_weight, out_weight
):
    gathered = lax.all_gather(own_rows, "expert", axis=0, tiled=True)
    count = gathered.shape[0]
    normed = rms_scale(gathered, gain)
    row_index = lax.axis_index("seq") * count + jnp.arange(count, dtype=jnp.int32)
    segment, place = positions(row_index, lengths, cached)
    gates = route_gates(normed, mixing, routes)
    experts = query_weight.shape[1]
    width = query_weight.shape[2]
    local_heads = width // HEAD_DIM
    query_all = jnp.dot(
        normed, query_weight.reshape(query_weight.shape[0], -1), preferred_element_type=jnp.float32
    )
    query_all = query_all.reshape(count, experts, local_heads, HEAD_DIM)
    query = jnp.take_along_axis(query_all, routes[:, :, None, None], axis=1)
    query = rotate(query, place).astype(jnp.bfloat16)
    queries = query.reshape(count * 2, local_heads, HEAD_DIM)
    projected = jnp.dot(
        normed, kv_weight.reshape(kv_weight.shape[0], -1), preferred_element_type=jnp.float32
    )
    projected = projected.reshape(count, 2, local_heads, HEAD_DIM)
    fresh_keys = rotate(projected[:, 0], place).astype(jnp.bfloat16).reshape(count, width)
    fresh_values = projected[:, 1].astype(jnp.bfloat16).reshape(count, width)
    fresh = jnp.stack([fresh_keys, fresh_values], axis=1)
    query_segment = jnp.repeat(segment, 2)
    query_index = jnp.repeat(row_index, 2)
    scale = HEAD_DIM ** (-0.5)
    slots = count * 2

    def absorb(carried, piece, allowed):
        row_top, row_total, row_sum = carried
        keys = piece[:, 0].reshape(-1, local_heads, HEAD_DIM)
        values = piece[:, 1].reshape(-1, local_heads, HEAD_DIM)
        scores = (
            jnp.einsum("qhd,khd->hqk", queries, keys, preferred_element_type=jnp.float32) * scale
        )
        scores = jnp.where(allowed[None], scores, NEGATIVE)
        new_top = jnp.maximum(row_top, jnp.max(scores, axis=2))
        weights = jnp.where(allowed[None], jnp.exp(scores - new_top[:, :, None]), 0.0)
        shrink = jnp.exp(row_top - new_top)
        row_total = row_total * shrink + jnp.sum(weights, axis=2)
        row_sum = row_sum * shrink[:, :, None] + jnp.einsum(
            "hqk,khd->hqd", weights.astype(jnp.bfloat16), values, preferred_element_type=jnp.float32
        )
        return (new_top, row_total, row_sum)

    initial = (
        jnp.full((local_heads, slots), NEGATIVE, jnp.float32),
        jnp.zeros((local_heads, slots), jnp.float32),
        jnp.zeros((local_heads, slots, HEAD_DIM), jnp.float32),
    )
    piece = lax.all_gather(cache_rows, "seq", axis=0, tiled=True)
    key_segment = segment_of(jnp.arange(piece.shape[0], dtype=jnp.int32), cached)
    allowed = query_segment[:, None] == key_segment[None, :]
    carried = absorb(initial, piece, allowed)
    piece = lax.all_gather(fresh, "seq", axis=0, tiled=True)
    key_index = jnp.arange(piece.shape[0], dtype=jnp.int32)
    key_segment = segment_of(key_index, lengths)
    allowed = (query_segment[:, None] == key_segment[None, :]) & (
        key_index[None, :] <= query_index[:, None]
    )
    row_top, row_total, row_sum = absorb(carried, piece, allowed)
    attended = (row_sum / row_total[:, :, None]).astype(jnp.bfloat16)
    attended = attended.transpose(1, 0, 2).reshape(count, 2, width)
    select = (routes[:, :, None] == jnp.arange(experts, dtype=jnp.int32)[None, None, :]).astype(
        jnp.float32
    )
    select = select * gates[:, :, None]
    spread = jnp.einsum("tka,tkd->tad", select, attended.astype(jnp.float32)).astype(jnp.bfloat16)
    spread = spread.reshape(count, experts * width)
    out_flat = out_weight.reshape(experts * width, -1)
    term = lax.psum_scatter(
        jnp.dot(spread, out_flat, preferred_element_type=jnp.float32).astype(jnp.bfloat16),
        "expert",
        scatter_dimension=0,
        tiled=True,
    ).astype(jnp.float32)
    return (own_rows.astype(jnp.float32) + term).astype(jnp.bfloat16)


def expert_hidden(rows, in_weight):
    single = in_weight[0]
    both = jnp.dot(rows, single.reshape(single.shape[0], -1), preferred_element_type=jnp.float32)
    both = both.reshape(rows.shape[0], 2, -1)
    return (jax.nn.silu(both[:, 0]) * both[:, 1]).astype(jnp.bfloat16)


def expert_block(middle, routes, gain, mixing, in_weight, down_weight):
    rows = middle.shape[0]
    features = middle.shape[1]
    normed = rms_scale(middle, gain)
    gates = route_gates(normed, mixing, routes)
    experts = mixing.shape[1]
    capacity = max(2, 4 * rows // experts)
    flat = routes.reshape(-1)
    member = (flat[:, None] == jnp.arange(experts, dtype=jnp.int32)[None, :]).astype(jnp.int32)
    earlier = jnp.cumsum(member, axis=0) - member
    slot = jnp.sum(earlier * member, axis=1)
    target = flat * capacity + slot
    table = (jnp.arange(experts * capacity, dtype=jnp.int32)[:, None] == target[None, :]).astype(
        jnp.bfloat16
    )
    table = jnp.sum(table.reshape(experts * capacity, rows, 2), axis=2)
    buffer = jnp.dot(table, normed, preferred_element_type=jnp.float32).astype(jnp.bfloat16)
    buffer = buffer.reshape(experts, capacity, features)
    seq_count = lax.axis_size("seq")
    copies = jnp.broadcast_to(buffer[None], (seq_count,) + buffer.shape)
    copies = copies.reshape(seq_count * experts, capacity, features)
    arrived = lax.all_to_all(copies, ("seq", "expert"), split_axis=0, concat_axis=0, tiled=True)
    flat_rows = arrived.reshape(-1, features)
    hidden = expert_hidden(flat_rows, in_weight)
    partial_value = jnp.dot(hidden, down_weight[0], preferred_element_type=jnp.float32)
    partial_value = partial_value.astype(jnp.bfloat16).reshape(arrived.shape)
    returned = lax.all_to_all(
        partial_value, ("seq", "expert"), split_axis=0, concat_axis=0, tiled=True
    )
    results = jnp.sum(
        returned.reshape(seq_count, experts, capacity, features).astype(jnp.float32), axis=0
    )
    picked = jnp.take(results.reshape(experts * capacity, features), target, axis=0).reshape(
        rows, 2, features
    )
    mixture = gates[:, 0:1] * picked[:, 0] + gates[:, 1:2] * picked[:, 1]
    return (middle.astype(jnp.float32) + mixture).astype(jnp.bfloat16)


def on_device(
    tokens,
    prompt_lengths,
    cache_lengths,
    kv_cache,
    attn_routes,
    ffn_routes,
    attn_gain,
    ffn_gain,
    attn_mix,
    query_weight,
    kv_weight,
    out_weight,
    ffn_mix,
    in_weight,
    down_weight,
):
    batch = lax.axis_index("section")
    middle = attention_block(
        select_batch(tokens, batch),
        select_batch(prompt_lengths, batch),
        select_batch(cache_lengths, batch),
        select_batch(kv_cache, batch),
        select_batch(attn_routes, batch),
        attn_gain,
        attn_mix,
        query_weight,
        kv_weight,
        out_weight,
    )
    finished = expert_block(
        middle, select_batch(ffn_routes, batch), ffn_gain, ffn_mix, in_weight, down_weight
    )
    return finished[None]


def solution(mesh):
    return jax.shard_map(
        on_device,
        mesh=mesh,
        in_specs=(
            P(None, ("seq", "expert"), None),
            P(),
            P(),
            P(None, "seq", None, "expert"),
            P(None, "seq", None),
            P(None, ("seq", "expert"), None),
            P(),
            P(),
            P(),
            P(None, None, "expert"),
            P(None, None, "expert"),
            P(None, "expert", None),
            P(),
            P("expert", None, None, "seq"),
            P("expert", "seq", None),
        ),
        out_specs=P("section", ("seq", "expert"), None),
        check_vma=False,
    )
```

profile of v0, /device:TPU:1, one launch (start us, length us, event | category | flops | bytes accessed | tf_op | source)
XLA Modules:
  0.0 283.1 jit_solution(11401811092933586299)
XLA Ops:
  8.2 15.0 %all-gather = bf16[1,128,2048]{2,1,0:T(8,128)(2,1)S(1)} all-gather(bf16[1,16,2048]{2,1,0:T(8,128)(2,1)S(1)} %constant_dynamic-slice_fusion.5), channel_id=2, replica_groups=mesh['section'=2,'seq'=8,'expert'=8] {'expert'}, dimensions={1}, use_global_device_ids=true | all-gather | bytes 589824 | tf_op jit(solution)/shard_map/all_gather | solution.py:60
  23.3 3.4 %copy.115 = bf16[256,8,2,256]{3,1,2,0:T(8,128)(2,1)} copy(bf16[256,8,2,256]{3,2,1,0:T(2,128)(2,1)} %bitcast.189) | data formatting | bytes 4194304
  26.7 4.0 %copy.97 = bf16[512,2048]{1,0:T(8,128)(2,1)} copy(bf16[512,2048]{0,1:T(8,128)(2,1)} %bitcast.186) | data formatting | bytes 4194304 | tf_op jit(solution)/shard_map/dot_general | solution.py:76
  30.7 2.4 fusion.42
  35.2 1.3 fusion.81
  39.4 1.5 pad_maximum_fusion.1
  41.0 1.8 constant_dynamic-slice_fusion.1
  42.8 1.8 copy.113
  44.7 1.5 copy.92
  46.2 1.5 copy.93
  48.3 2.4 gather_fusion.1
  51.0 5.2 %copy.114 = bf16[256,8,4,256]{3,1,2,0:T(8,128)(2,1)} copy(bf16[256,8,4,256]{3,2,1,0:T(4,128)(2,1)} %bitcast.187) | data formatting | bytes 8388608
  56.2 6.5 %copy.89 = bf16[1024,2048]{1,0:T(8,128)(2,1)} copy(bf16[1024,2048]{0,1:T(8,128)(2,1)} %bitcast.183) | data formatting | bytes 8388608 | tf_op jit(solution)/shard_map/dot_general | solution.py:69
  62.7 3.7 %fusion.44 = f32[128,4,2,128]{3,0,2,1:T(8,128)S(1)} fusion(bf16[4,2,128,2048]{3,2,1,0:T(8,128)(2,1)} %bitcast.182, bf16[1,128,2048]{2,1,0:T(8,128)(2,1)S(1)} %all-gather, f32[2048]{0:T(1024)S(1)} %copy-done.12, f32[128]{0:T(128)S(1)} %copy-done.23), kind=kOutput, calls=%fused_computation.52 | convolution fusion | flops 537919488 | bytes 5251584 | tf_op jit(solution)/shard_map/dot_general | solution.py:69
  66.9 1.9 gather_fusion.2
  73.4 2.0 subtract_convert_fusion
  75.7 5.5 %all-gather.5.cloned.1.call-done = bf16[1024,2,256]{0,2,1:T(8,128)(2,1)} async-done(((bf16[128,2,256]{0,2,1:T(8,128)(2,1)}), bf16[1024,2,256]{0,2,1:T(8,128)(2,1)}) %all-gather.5.cloned.1.call-update) | async-done | bytes 1048592 | tf_op jit(solution)/shard_map/all_gather | solution.py:114
  81.2 2.1 fusion.105
  83.3 2.0 fusion.15
  85.3 59.9 %all-gather.7.cloned.1.call-done = bf16[1,2048,2,256]{1,3,2,0:T(8,128)(2,1)} async-done(((bf16[1,256,2,256]{1,3,2,0:T(8,128)(2,1)}), bf16[1,2048,2,256]{1,3,2,0:T(8,128)(2,1)}) %all-gather.7.cloned.1.call-update) | async-done | bytes 2097168 | tf_op jit(solution)/shard_map/all_gather | solution.py:110
  145.3 1.8 fusion.104
  148.3 1.4 fusion.3
  150.7 1.4 fusion.27
  154.0 3.7 %fusion.9 = bf16[128,2048]{1,0:T(8,128)(2,1)} fusion(bf16[4,256,2048]{2,1,0:T(8,128)(2,1)} %param.26, bf16[128,4,256]{2,1,0:T(4,128)(2,1)S(1)} %convolution_convert_fusion.2), kind=kOutput, calls=%fused_computation.16 | convolution fusion | flops 537133056 | bytes 4980736 | tf_op jit(solution)/shard_map/dot_general | solution.py:131
  158.7 30.2 %reduce-scatter.2.cloned.1.call-done = bf16[16,2048]{1,0:T(8,128)(2,1)} async-done(((bf16[128,2048]{1,0:T(8,128)(2,1)}), bf16[16,2048]{1,0:T(8,128)(2,1)}) %reduce-scatter.2.cloned.1.call-update) | async-done | bytes 65552 | tf_op jit(solution)/shard_map/reduce_scatter | solution.py:130
  190.4 38.1 %all_to_all.10 = bf16[64,8,2048]{2,1,0:T(8,128)(2,1)S(1)} all-to-all(bf16[64,8,2048]{2,1,0:T(8,128)(2,1)S(1)} %bitcast.185), channel_id=1, replica_groups=mesh['section'=2,'seq'=8,'expert'=8] {'seq','expert'}, dimensions={0} | all-to-all | bytes 4194304 | tf_op jit(solution)/shard_map/all_to_all | solution.py:167
  228.5 5.2 %fusion = f32[512,2,704]{0,2,1:T(8,128)S(1)} fusion(bf16[1,2048,2,704]{1,3,2,0:T(8,128)(2,1)} %param.28, bf16[64,8,2048]{2,1,0:T(8,128)(2,1)S(1)} %all_to_all.10), kind=kOutput, calls=%fused_computation.4 | convolution fusion | flops 2952790016 | bytes 10747904 | tf_op jit(solution)/shard_map/dot_general | solution.py:141
  233.7 3.3 %fusion.6 = bf16[64,8,2048]{2,1,0:T(8,128)(2,1)} fusion(bf16[1,704,2048]{2,1,0:T(8,128)(2,1)S(1)} %copy-done, f32[512,2,704]{0,2,1:T(8,128)S(1)} %fusion), kind=kOutput, calls=%fused_computation.14 | convolution fusion | flops 1479606272 | bytes 7864320 | tf_op jit(solution)/shard_map/dot_general | solution.py:170
  237.0 5.3 %all-to-all-start.1 = ((bf16[64,8,2048]{2,1,0:T(8,128)(2,1)}), bf16[64,8,2048]{2,1,0:T(8,128)(2,1)}, u32[]{:S(2)}, u32[]{:S(2)}) async-start(bf16[64,8,2048]{2,1,0:T(8,128)(2,1)} %fusion.6), calls=%async_computation.2 | async-start | bytes 4194304 | tf_op jit(solution)/shard_map/all_to_all | solution.py:172
  243.8 27.5 %all-to-all-done.1 = bf16[64,8,2048]{2,1,0:T(8,128)(2,1)} async-done(((bf16[64,8,2048]{2,1,0:T(8,128)(2,1)}), bf16[64,8,2048]{2,1,0:T(8,128)(2,1)}, u32[]{:S(2)}, u32[]{:S(2)}) %all-to-all-start.1) | async-done | bytes 2097184 | tf_op jit(solution)/shard_map/all_to_all | solution.py:172
  271.2 2.0 convert_reduce_fusion
  273.3 1.3 gather_fusion
  (136 shorter events, 23.1 us)
Async XLA Ops:
  6.5 227.2 %copy-start = (bf16[1,704,2048]{2,1,0:T(8,128)(2,1)S(1)}, bf16[1,704,2048]{2,1,0:T(8,128)(2,1)}, u32[]{:S(2)}) copy-start(bf16[1,704,2048]{2,1,0:T(8,128)(2,1)} %param.29) | copy-start | bytes 8650756
  6.5 74.7 %all-gather.5.cloned.1.call-start = ((), (), s32[]{:S(2)}) async-start(), calls=%async_computation.3 | async-start | bytes 1179648 | tf_op jit(solution)/shard_map/all_gather | solution.py:114
  23.3 7.4 %copy-start.22 = (f32[128]{0:T(128)}, f32[128]{0:T(128)S(1)}, u32[]{:S(2)}) copy-start(f32[128]{0:T(128)S(1)} %add_rsqrt_fusion.1) | copy-start | bytes 1540
  26.7 4.0 %copy-start.12 = (f32[2048]{0:T(1024)S(1)}, f32[2048]{0:T(1024)}, u32[]{:S(2)}) copy-start(f32[2048]{0:T(1024)} %param.21) | copy-start | bytes 24580
  30.7 3.1 %copy-start.17 = (s32[2,3]{1,0:T(2,128)S(1)}, s32[2,3]{1,0:T(2,128)}, u32[]{:S(2)}) copy-start(s32[2,3]{1,0:T(2,128)} %param.16) | copy-start | bytes 76
  30.7 3.1 %copy-start.24 = (s32[2,3]{1,0:T(2,128)S(1)}, s32[2,3]{1,0:T(2,128)}, u32[]{:S(2)}) copy-start(s32[2,3]{1,0:T(2,128)} %param.17) | copy-start | bytes 76
  33.1 14.6 %copy-start.14 = (s32[2,128,2]{1,2,0:T(2,128)S(1)}, s32[2,128,2]{1,2,0:T(2,128)}, u32[]{:S(2)}) copy-start(s32[2,128,2]{1,2,0:T(2,128)} %param.19) | copy-start | bytes 6148
  35.2 1.3 copy-start.15
  36.5 0.8 copy-start.18
  38.8 0.6 copy-start.7
  38.8 0.6 copy-start.8
  39.4 8.5 %copy-start.23 = (f32[128]{0:T(128)S(1)}, f32[128]{0:T(128)}, u32[]{:S(2)}) copy-start(f32[128]{0:T(128)} %copy-done.22) | copy-start | bytes 1540
  39.4 8.6 %copy-start.26 = (bf16[2048,4]{0,1:T(4,128)(2,1)S(1)}, bf16[2048,4]{0,1:T(4,128)(2,1)}, u32[]{:S(2)}) copy-start(bf16[2048,4]{0,1:T(4,128)(2,1)} %param.23) | copy-start | bytes 49156
  41.0 104.3 %all-gather.7.cloned.1.call-start = ((), (), s32[]{:S(2)}) async-start(), calls=%async_computation.5 | async-start | bytes 2359296 | tf_op jit(solution)/shard_map/all_gather | solution.py:110
  44.7 144.2 %reduce-scatter.2.cloned.1.call-start = ((), (), s32[]{:S(2)}) async-start(), calls=%async_computation.4 | async-start | bytes 589824 | tf_op jit(solution)/shard_map/reduce_scatter | solution.py:130
  62.7 6.3 %copy-start.19 = (s32[128]{0:T(128)S(1)}, s32[128]{0:T(128)}, u32[]{:S(2)}) copy-start(s32[128]{0:T(128)} %copy-done.18) | copy-start | bytes 1540
  62.7 6.6 %copy-start.21 = (s32[3,1]{0,1:T(1,128)S(1)}, s32[3,1]{0,1:T(1,128)}, u32[]{:S(2)}) copy-start(s32[3,1]{0,1:T(1,128)} %get-tuple-element.33) | copy-start | bytes 40
  62.7 8.2 %copy-start.16 = (s32[3,1]{0,1:T(1,128)S(1)}, s32[3,1]{0,1:T(1,128)}, u32[]{:S(2)}) copy-start(s32[3,1]{0,1:T(1,128)} %copy-done.15) | copy-start | bytes 40
  81.2 2.1 copy-start.2
  81.2 2.1 copy-start.4
  145.3 1.8 copy-start.5
  148.3 1.6 copy-start.1
  148.3 1.6 copy-start.3
  150.7 1.4 copy-start.6
  152.2 1.1 copy-start.10
  152.2 1.1 copy-start.11
  153.9 3.8 %copy-start.20 = (s32[2,16,2]{1,2,0:T(2,128)S(1)}, s32[2,16,2]{1,2,0:T(2,128)}, u32[]{:S(2)}) copy-start(s32[2,16,2]{1,2,0:T(2,128)} %param.20) | copy-start | bytes 772
  153.9 34.9 %copy-start.9 = (bf16[2,16,2048]{2,1,0:T(8,128)(2,1)S(1)}, bf16[2,16,2048]{2,1,0:T(8,128)(2,1)}, u32[]{:S(2)}) copy-start(bf16[2,16,2048]{2,1,0:T(8,128)(2,1)} %param.15) | copy-start | bytes 393220
  153.9 35.9 %copy-start.13 = (f32[2048]{0:T(1024)S(1)}, f32[2048]{0:T(1024)}, u32[]{:S(2)}) copy-start(f32[2048]{0:T(1024)} %param.22) | copy-start | bytes 24580
  237.0 5.7 %copy-start.25 = (bf16[2048,8]{0,1:T(8,128)(2,1)S(1)}, bf16[2048,8]{0,1:T(8,128)(2,1)}, u32[]{:S(2)}) copy-start(bf16[2048,8]{0,1:T(8,128)(2,1)} %param.27) | copy-start | bytes 98308
  237.0 34.2 %all-to-all-start.1 = ((bf16[64,8,2048]{2,1,0:T(8,128)(2,1)}), bf16[64,8,2048]{2,1,0:T(8,128)(2,1)}, u32[]{:S(2)}, u32[]{:S(2)}) async-start(bf16[64,8,2048]{2,1,0:T(8,128)(2,1)} %fusion.6), calls=%async_computation.2 | async-start | bytes 4194304 | tf_op jit(solution)/shard_map/all_to_all | solution.py:172
Sparse Core Ops, SparseCore 0:
  41.1 40.0 all-gather.4
  82.8 62.4 all-gather.6
  157.8 31.0 reduce-scatter.1
where the time goes:
time: 284 us; the launch traced here: 283 us
  waiting for transfers between devices  123 us (43%)
  blocking collectives  53 us (19%)
  local copies, waits for them, and re-layouts  44.3 us (16%)
  matrix products  25.3 us (9%)
  other arithmetic  18.4 us (6%)
  between operations  13.6 us (5%)
  starting transfers between devices  5.34 us (2%)
    all_gather x1, waiting for transfers between devices, attention_block(): piece = lax.all_gather(cache_rows, 'seq', axis=0, tiled=True)  59.9 us
    all_to_all x1, blocking collectives, expert_block(): lax.all_to_all(copies, ('seq', 'expert'), split_axis=0, concat_axis=0, ti...  38.1 us
    reduce_scatter x1, waiting for transfers between devices, attention_block(): lax.psum_scatter(jnp.dot(spread, out_flat, preferred_element_type=jnp.flo...  30.2 us
    all_to_all x1, waiting for transfers between devices, expert_block(): lax.all_to_all(partial_value, ('seq', 'expert'), split_axis=0, concat_axi...  27.5 us
    all_gather x1, blocking collectives, attention_block(): gathered = lax.all_gather(own_rows, 'expert', axis=0, tiled=True)  15 us
    unnamed x57, local copies, waits for them, and re-layouts  11.2 us
    dot_general x2, local copies, waits for them, and re-layouts, attention_block(): jnp.dot(normed, query_weight.reshape(query_weight.shape[0], -1), preferre...  6.91 us
  transfers between devices with their start and end apart: 4, of which 4 were waited for; matrix products, arithmetic and copies ran while one was open for 14% of the time, Pallas kernels for 0%

commit v1 on v0

--- a/solution.py
+++ b/solution.py
@@ -57,7 +57,14 @@
 def attention_block(
     own_rows, lengths, cached, cache_rows, routes, gain, mixing, query_weight, kv_weight, out_weight
 ):
-    gathered = lax.all_gather(own_rows, "expert", axis=0, tiled=True)
+    ring = [own_rows]
+    for hop in range(7):
+        ring.append(lax.ppermute(ring[-1], "expert", [(dev, (dev + 1) % 8) for dev in range(8)]))
+    gathered = jnp.roll(
+        jnp.concatenate(ring[::-1], axis=0),
+        (lax.axis_index("expert") + 1) * ring[0].shape[0],
+        axis=0,
+    )
     count = gathered.shape[0]
     normed = rms_scale(gathered, gain)
     row_index = lax.axis_index("seq") * count + jnp.arange(count, dtype=jnp.int32)

time: 284 us -> 293 us (1.032)
  waiting for transfers between devices: 123 us -> 143 us
  blocking collectives: 53 us -> 38 us
  starting transfers between devices: 5.34 us -> 14.3 us
  other arithmetic: 18.4 us -> 13.7 us
    ppermute x0 -> x7, waiting for transfers between devices: none -> 15.4 us  [attention_block(): lax.ppermute(ring[-1], 'expert', [(dev, (dev + 1) % 8) for dev in range(8)])]
    all_gather x1 -> x0, blocking collectives: 15 us -> none  [attention_block(): gathered = lax.all_gather(own_rows, 'expert', axis=0, tiled=True)]
    ppermute x0 -> x7, starting transfers between devices: none -> 9 us  [attention_block(): lax.ppermute(ring[-1], 'expert', [(dev, (dev + 1) % 8) for dev in range(8)])]
    all_gather x1, waiting for transfers between devices: 5.47 us -> 10 us  [attention_block(): piece = lax.all_gather(fresh, 'seq', axis=0, tiled=True)]
    unnamed x57 -> x62, local copies, waits for them, and re-layouts: 11.2 us -> 11.3 us
  transfers between devices with their start and end apart: 4 -> 11, of which waited for: 4 -> 9; matrix products, arithmetic and copies ran while one was open for 14% -> 17% of each run, Pallas kernels for 0% -> 0%
where the time goes in v1:
time: 293 us; the launch traced here: 292 us
  waiting for transfers between devices  143 us (49%)
  local copies, waits for them, and re-layouts  44.2 us (15%)
  blocking collectives  38 us (13%)
  matrix products  24.9 us (8%)
  starting transfers between devices  14.3 us (5%)
  other arithmetic  13.7 us (5%)
  between operations  13.7 us (5%)
    all_gather x1, waiting for transfers between devices, attention_block(): piece = lax.all_gather(cache_rows, 'seq', axis=0, tiled=True)  59.9 us
    all_to_all x1, blocking collectives, expert_block(): lax.all_to_all(copies, ('seq', 'expert'), split_axis=0, concat_axis=0, ti...  38 us
    reduce_scatter x1, waiting for transfers between devices, attention_block(): lax.psum_scatter(jnp.dot(spread, out_flat, preferred_element_type=jnp.flo...  30.3 us
    all_to_all x1, waiting for transfers between devices, expert_block(): lax.all_to_all(partial_value, ('seq', 'expert'), split_axis=0, concat_axi...  27.5 us
    ppermute x7, waiting for transfers between devices, attention_block(): lax.ppermute(ring[-1], 'expert', [(dev, (dev + 1) % 8) for dev in range(8)])  15.4 us
    unnamed x62, local copies, waits for them, and re-layouts  11.3 us
    all_gather x1, waiting for transfers between devices, attention_block(): piece = lax.all_gather(fresh, 'seq', axis=0, tiled=True)  10 us
    ppermute x7, starting transfers between devices, attention_block(): lax.ppermute(ring[-1], 'expert', [(dev, (dev + 1) % 8) for dev in range(8)])  9 us
  transfers between devices with their start and end apart: 11, of which 9 were waited for; matrix products, arithmetic and copies ran while one was open for 17% of the time, Pallas kernels for 0%

profile of v1, /device:TPU:1, one launch (start us, length us, event | category | flops | bytes accessed | tf_op | source)
XLA Modules:
  0.0 292.0 jit_solution(3320408799898428710)
XLA Ops:
  7.5 2.7 collective-permute-start
  12.3 1.6 collective-permute-start.1
  15.2 2.4 collective-permute-start.2
  17.7 1.8 collective-permute-done.2
  19.5 1.8 collective-permute-start.3
  21.4 3.0 %collective-permute-done.3 = bf16[16,2048]{1,0:T(8,128)(2,1)S(1)} collective-permute-done((bf16[16,2048]{1,0:T(8,128)(2,1)S(1)}, bf16[16,2048]{1,0:T(8,128)(2,1)S(1)}, u32[]{:S(2)}, u32[]{:S(2)}) %collective-permute-start.3) | collective-permute-done | bytes 65568 | tf_op jit(solution)/shard_map/ppermute | solution.py:62
  25.0 4.3 %collective-permute-done.4 = bf16[16,2048]{1,0:T(8,128)(2,1)S(1)} collective-permute-done((bf16[16,2048]{1,0:T(8,128)(2,1)S(1)}, bf16[16,2048]{1,0:T(8,128)(2,1)S(1)}, u32[]{:S(2)}, u32[]{:S(2)}) %collective-permute-start.4) | collective-permute-done | bytes 65568 | tf_op jit(solution)/shard_map/ppermute | solution.py:62
  29.3 4.9 %collective-permute-done.5 = bf16[16,2048]{1,0:T(8,128)(2,1)S(1)} collective-permute-done((bf16[16,2048]{1,0:T(8,128)(2,1)S(1)}, bf16[16,2048]{1,0:T(8,128)(2,1)S(1)}, u32[]{:S(2)}, u32[]{:S(2)}) %collective-permute-start.5) | collective-permute-done | bytes 65568 | tf_op jit(solution)/shard_map/ppermute | solution.py:62
  34.4 3.3 %copy.115 = bf16[256,8,2,256]{3,1,2,0:T(8,128)(2,1)} copy(bf16[256,8,2,256]{3,2,1,0:T(2,128)(2,1)} %bitcast.182) | data formatting | bytes 4194304
  37.8 4.0 %copy.97 = bf16[512,2048]{1,0:T(8,128)(2,1)} copy(bf16[512,2048]{0,1:T(8,128)(2,1)} %bitcast.179) | data formatting | bytes 4194304 | tf_op jit(solution)/shard_map/dot_general | solution.py:83
  49.2 5.2 %copy.114 = bf16[256,8,4,256]{3,1,2,0:T(8,128)(2,1)} copy(bf16[256,8,4,256]{3,2,1,0:T(4,128)(2,1)} %bitcast.180) | data formatting | bytes 8388608
  54.4 6.5 %copy.89 = bf16[1024,2048]{1,0:T(8,128)(2,1)} copy(bf16[1024,2048]{0,1:T(8,128)(2,1)} %bitcast.176) | data formatting | bytes 8388608 | tf_op jit(solution)/shard_map/dot_general | solution.py:76
  63.2 1.4 fusion.97
  64.6 2.6 gather_fusion.1
  68.3 3.9 %fusion.44 = f32[128,4,2,128]{3,0,2,1:T(8,128)S(1)} fusion(bf16[4,2,128,2048]{3,2,1,0:T(8,128)(2,1)} %bitcast.175, f32[2048]{0:T(1024)S(1)} %copy-done.13, f32[128]{0:T(128)S(1)} %add_rsqrt_fusion.1, bf16[256,2048]{1,0:T(8,128)(2,1)} %copy-done.5, s32[]{:T(128)S(6)} %select_n.125), kind=kOutput, calls=%fused_computation.52 | convolution fusion | flops 537919488 | bytes 5251588 | tf_op jit(solution)/shard_map/dot_general | solution.py:76
  73.4 3.0 %gather_fusion.2 = f32[256,2,128]{2,1,0:T(2,128)} fusion(f32[128,4,2,128]{3,2,1,0:T(2,128)} %copy.90, s32[256]{0:T(256)S(1)} %reshape.544), kind=kCustom, calls=%fused_computation.2 | custom fusion | bytes 526336 | tf_op jit(solution)/shard_map/jit(take_along_axis)/gather | solution.py:80
  78.2 2.0 subtract_convert_fusion
  80.2 10.0 %all-gather.4.cloned.1.call-done = bf16[1024,2,256]{0,2,1:T(8,128)(2,1)} async-done(((bf16[128,2,256]{0,2,1:T(8,128)(2,1)}), bf16[1024,2,256]{0,2,1:T(8,128)(2,1)}) %all-gather.4.cloned.1.call-update) | async-done | bytes 1048592 | tf_op jit(solution)/shard_map/all_gather | solution.py:121
  90.2 2.1 fusion.103
  92.4 2.0 fusion.15
  94.3 59.9 %all-gather.6.cloned.1.call-done = bf16[1,2048,2,256]{1,3,2,0:T(8,128)(2,1)} async-done(((bf16[1,256,2,256]{1,3,2,0:T(8,128)(2,1)}), bf16[1,2048,2,256]{1,3,2,0:T(8,128)(2,1)}) %all-gather.6.cloned.1.call-update) | async-done | bytes 2097168 | tf_op jit(solution)/shard_map/all_gather | solution.py:117
  154.2 1.8 fusion.102
  157.2 1.4 fusion.3
  159.7 1.4 fusion.27
  162.9 3.7 %fusion.9 = bf16[128,2048]{1,0:T(8,128)(2,1)} fusion(bf16[4,256,2048]{2,1,0:T(8,128)(2,1)} %param.26, bf16[128,4,256]{2,1,0:T(4,128)(2,1)S(1)} %convolution_convert_fusion.2), kind=kOutput, calls=%fused_computation.16 | convolution fusion | flops 537133056 | bytes 4980736 | tf_op jit(solution)/shard_map/dot_general | solution.py:138
  167.4 30.3 %reduce-scatter.2.cloned.1.call-done = bf16[16,2048]{1,0:T(8,128)(2,1)} async-done(((bf16[128,2048]{1,0:T(8,128)(2,1)}), bf16[16,2048]{1,0:T(8,128)(2,1)}) %reduce-scatter.2.cloned.1.call-update) | async-done | bytes 65552 | tf_op jit(solution)/shard_map/reduce_scatter | solution.py:137
  199.3 38.0 %all_to_all.10 = bf16[64,8,2048]{2,1,0:T(8,128)(2,1)S(1)} all-to-all(bf16[64,8,2048]{2,1,0:T(8,128)(2,1)S(1)} %bitcast.178), channel_id=1, replica_groups=mesh['section'=2,'seq'=8,'expert'=8] {'seq','expert'}, dimensions={0} | all-to-all | bytes 4194304 | tf_op jit(solution)/shard_map/all_to_all | solution.py:174
  237.3 5.2 %fusion = f32[512,2,704]{0,2,1:T(8,128)S(1)} fusion(bf16[1,2048,2,704]{1,3,2,0:T(8,128)(2,1)} %param.28, bf16[64,8,2048]{2,1,0:T(8,128)(2,1)S(1)} %all_to_all.10), kind=kOutput, calls=%fused_computation.4 | convolution fusion | flops 2952790016 | bytes 10747904 | tf_op jit(solution)/shard_map/dot_general | solution.py:148
  242.6 3.3 %fusion.6 = bf16[64,8,2048]{2,1,0:T(8,128)(2,1)} fusion(bf16[1,704,2048]{2,1,0:T(8,128)(2,1)S(1)} %copy-done, f32[512,2,704]{0,2,1:T(8,128)S(1)} %fusion), kind=kOutput, calls=%fused_computation.14 | convolution fusion | flops 1479606272 | bytes 7864320 | tf_op jit(solution)/shard_map/dot_general | solution.py:177
  245.9 5.3 %all-to-all-start.1 = ((bf16[64,8,2048]{2,1,0:T(8,128)(2,1)}), bf16[64,8,2048]{2,1,0:T(8,128)(2,1)}, u32[]{:S(2)}, u32[]{:S(2)}) async-start(bf16[64,8,2048]{2,1,0:T(8,128)(2,1)} %fusion.6), calls=%async_computation.2 | async-start | bytes 4194304 | tf_op jit(solution)/shard_map/all_to_all | solution.py:179
  252.6 27.5 %all-to-all-done.1 = bf16[64,8,2048]{2,1,0:T(8,128)(2,1)} async-done(((bf16[64,8,2048]{2,1,0:T(8,128)(2,1)}), bf16[64,8,2048]{2,1,0:T(8,128)(2,1)}, u32[]{:S(2)}, u32[]{:S(2)}) %all-to-all-start.1) | async-done | bytes 2097184 | tf_op jit(solution)/shard_map/all_to_all | solution.py:179
  280.1 2.0 convert_reduce_fusion
  (155 shorter events, 30.0 us)
Async XLA Ops:
  6.5 236.0 %copy-start = (bf16[1,704,2048]{2,1,0:T(8,128)(2,1)S(1)}, bf16[1,704,2048]{2,1,0:T(8,128)(2,1)}, u32[]{:S(2)}) copy-start(bf16[1,704,2048]{2,1,0:T(8,128)(2,1)} %param.29) | copy-start | bytes 8650756
  6.5 83.7 %all-gather.4.cloned.1.call-start = ((), (), s32[]{:S(2)}) async-start(), calls=%async_computation.3 | async-start | bytes 1179648 | tf_op jit(solution)/shard_map/all_gather | solution.py:121
  7.5 4.8 %collective-permute-start = (bf16[16,2048]{1,0:T(8,128)(2,1)S(1)}, bf16[16,2048]{1,0:T(8,128)(2,1)S(1)}, u32[]{:S(2)}, u32[]{:S(2)}) collective-permute-start(bf16[16,2048]{1,0:T(8,128)(2,1)S(1)} %dynamic-slice_bitcast_fusion), channel_id=1, source_target_pairs={{0,1},{1,2},{2,3},{3,4},{4,5},{5,6},{6,7},{7,0},{8,9},{9,10},{10,1... | collective-permute-start | bytes 196616 | tf_op jit(solution)/shard_map/ppermute | solution.py:62
  12.3 2.9 collective-permute-start.1
  13.9 7.4 %copy-start.16 = (s32[128]{0:T(128)}, s32[128]{0:T(128)S(1)}, u32[]{:S(2)}) copy-start(s32[128]{0:T(128)S(1)} %iota_add_fusion) | copy-start | bytes 1540
  15.2 4.3 %collective-permute-start.2 = (bf16[16,2048]{1,0:T(8,128)(2,1)S(1)}, bf16[16,2048]{1,0:T(8,128)(2,1)S(1)}, u32[]{:S(2)}, u32[]{:S(2)}) collective-permute-start(bf16[16,2048]{1,0:T(8,128)(2,1)S(1)} %collective-permute-done.1), channel_id=1, source_target_pairs={{0,1},{1,2},{2,3},{3,4},{4,5},{5,6},{6,7},{7,0},{8,9},{9,10},{10,1... | collective-permute-start | bytes 196616 | tf_op jit(solution)/shard_map/ppermute | solution.py:62
  19.5 4.9 %collective-permute-start.3 = (bf16[16,2048]{1,0:T(8,128)(2,1)S(1)}, bf16[16,2048]{1,0:T(8,128)(2,1)S(1)}, u32[]{:S(2)}, u32[]{:S(2)}) collective-permute-start(bf16[16,2048]{1,0:T(8,128)(2,1)S(1)} %collective-permute-done.2), channel_id=1, source_target_pairs={{0,1},{1,2},{2,3},{3,4},{4,5},{5,6},{6,7},{7,0},{8,9},{9,10},{10,1... | collective-permute-start | bytes 196616 | tf_op jit(solution)/shard_map/ppermute | solution.py:62
  24.4 4.9 %collective-permute-start.4 = (bf16[16,2048]{1,0:T(8,128)(2,1)S(1)}, bf16[16,2048]{1,0:T(8,128)(2,1)S(1)}, u32[]{:S(2)}, u32[]{:S(2)}) collective-permute-start(bf16[16,2048]{1,0:T(8,128)(2,1)S(1)} %collective-permute-done.3), channel_id=1, source_target_pairs={{0,1},{1,2},{2,3},{3,4},{4,5},{5,6},{6,7},{7,0},{8,9},{9,10},{10,1... | collective-permute-start | bytes 196616 | tf_op jit(solution)/shard_map/ppermute | solution.py:62
  29.3 4.9 %collective-permute-start.5 = (bf16[16,2048]{1,0:T(8,128)(2,1)S(1)}, bf16[16,2048]{1,0:T(8,128)(2,1)S(1)}, u32[]{:S(2)}, u32[]{:S(2)}) collective-permute-start(bf16[16,2048]{1,0:T(8,128)(2,1)S(1)} %collective-permute-done.4), channel_id=1, source_target_pairs={{0,1},{1,2},{2,3},{3,4},{4,5},{5,6},{6,7},{7,0},{8,9},{9,10},{10,1... | collective-permute-start | bytes 196616 | tf_op jit(solution)/shard_map/ppermute | solution.py:62
  34.2 7.6 %collective-permute-start.6 = (bf16[16,2048]{1,0:T(8,128)(2,1)S(1)}, bf16[16,2048]{1,0:T(8,128)(2,1)S(1)}, u32[]{:S(2)}, u32[]{:S(2)}) collective-permute-start(bf16[16,2048]{1,0:T(8,128)(2,1)S(1)} %collective-permute-done.5), channel_id=1, source_target_pairs={{0,1},{1,2},{2,3},{3,4},{4,5},{5,6},{6,7},{7,0},{8,9},{9,10},{10,1... | collective-permute-start | bytes 196616 | tf_op jit(solution)/shard_map/ppermute | solution.py:62
  37.8 4.1 %copy-start.8 = (bf16[2,16,2048]{2,1,0:T(8,128)(2,1)S(1)}, bf16[2,16,2048]{2,1,0:T(8,128)(2,1)}, u32[]{:S(2)}) copy-start(bf16[2,16,2048]{2,1,0:T(8,128)(2,1)} %param.15) | copy-start | bytes 393220
  41.8 2.0 copy-start.4
  42.1 2.6 copy-start.5
  43.8 5.2 %copy-start.15 = (s32[2,128,2]{1,2,0:T(2,128)S(1)}, s32[2,128,2]{1,2,0:T(2,128)}, u32[]{:S(2)}) copy-start(s32[2,128,2]{1,2,0:T(2,128)} %param.19) | copy-start | bytes 6148
  45.4 108.8 %all-gather.6.cloned.1.call-start = ((), (), s32[]{:S(2)}) async-start(), calls=%async_computation.5 | async-start | bytes 2359296 | tf_op jit(solution)/shard_map/all_gather | solution.py:117
  47.5 150.3 %reduce-scatter.2.cloned.1.call-start = ((), (), s32[]{:S(2)}) async-start(), calls=%async_computation.4 | async-start | bytes 589824 | tf_op jit(solution)/shard_map/reduce_scatter | solution.py:137
  54.4 6.7 %copy-start.17 = (s32[128]{0:T(128)S(1)}, s32[128]{0:T(128)}, u32[]{:S(2)}) copy-start(s32[128]{0:T(128)} %copy-done.16) | copy-start | bytes 1540
  54.4 7.0 %copy-start.19 = (s32[3,1]{0,1:T(1,128)S(1)}, s32[3,1]{0,1:T(1,128)}, u32[]{:S(2)}) copy-start(s32[3,1]{0,1:T(1,128)} %get-tuple-element.33) | copy-start | bytes 40
  54.4 8.8 %copy-start.21 = (bf16[2048,4]{0,1:T(4,128)(2,1)S(1)}, bf16[2048,4]{0,1:T(4,128)(2,1)}, u32[]{:S(2)}) copy-start(bf16[2048,4]{0,1:T(4,128)(2,1)} %param.23) | copy-start | bytes 49156
  90.2 2.1 copy-start.2
  90.2 2.1 copy-start.6
  154.2 1.8 copy-start.7
  157.2 1.6 copy-start.1
  157.2 1.6 copy-start.3
  159.7 1.4 copy-start.10
  161.1 1.1 copy-start.11
  161.1 1.1 copy-start.12
  162.8 3.8 %copy-start.18 = (s32[2,16,2]{1,2,0:T(2,128)S(1)}, s32[2,16,2]{1,2,0:T(2,128)}, u32[]{:S(2)}) copy-start(s32[2,16,2]{1,2,0:T(2,128)} %param.20) | copy-start | bytes 772
  162.9 34.9 %copy-start.9 = (bf16[2,16,2048]{2,1,0:T(8,128)(2,1)S(1)}, bf16[2,16,2048]{2,1,0:T(8,128)(2,1)}, u32[]{:S(2)}) copy-start(bf16[2,16,2048]{2,1,0:T(8,128)(2,1)} %param.15) | copy-start | bytes 393220
  162.9 35.9 %copy-start.14 = (f32[2048]{0:T(1024)S(1)}, f32[2048]{0:T(1024)}, u32[]{:S(2)}) copy-start(f32[2048]{0:T(1024)} %param.22) | copy-start | bytes 24580
  245.9 5.7 %copy-start.20 = (bf16[2048,8]{0,1:T(8,128)(2,1)S(1)}, bf16[2048,8]{0,1:T(8,128)(2,1)}, u32[]{:S(2)}) copy-start(bf16[2048,8]{0,1:T(8,128)(2,1)} %param.27) | copy-start | bytes 98308
  245.9 34.2 %all-to-all-start.1 = ((bf16[64,8,2048]{2,1,0:T(8,128)(2,1)}), bf16[64,8,2048]{2,1,0:T(8,128)(2,1)}, u32[]{:S(2)}, u32[]{:S(2)}) async-start(bf16[64,8,2048]{2,1,0:T(8,128)(2,1)} %fusion.6), calls=%async_computation.2 | async-start | bytes 4194304 | tf_op jit(solution)/shard_map/all_to_all | solution.py:179
  (1 other events, 0.7 us)
Sparse Core Ops, SparseCore 0:
  45.5 44.7 all-gather.3
  91.8 62.3 all-gather.5
  166.8 30.9 reduce-scatter.1
